TPU v7x, 256 devices: a whole 4x4x8 slice. The times are simulated.
256 devices in a mesh: scen: 64 (over y, z, core), link: 4 (over x).
Axes of the slice: x: 4, y: 4, z: 8, core: 2. Of those that a mesh axis runs over, the one named last changes fastest.
Arguments:
- factor_inv: bfloat16 [128, 1024, 1024], P('scen'), may hold values from -0.1875 to 0.1875
- coupling: bfloat16 [128, 1024, 1024], P('scen', None, 'link'), may hold values from -0.375 to 0.375
- first_diag: float32 [128, 128], P('scen'), may hold values from 1 to 10
- pattern: int32 [128, 8], P('scen'), may hold values from 0 to 127, as said below
Outputs:
- panel: float32 [16384, 128], P('scen')
- trailing: float32 [16384, 16384], P('scen', 'link')
Inputs may be any that keep to these rules, and one draw needn't show every extreme that they name: `pattern`: slot t of a scenario names a block of column range t // 2, that is, a block p with p // 32 = t // 2. The 2 scenarios of rows s * 2 to (s + 1) * 2 - 1 name every block at most once among them, and at most 1 block of any one group of blocks with the same p // 2. The first scenario of every such set names block 0 in slot 0.
All inputs are finite; a program needn't handle non-finite values.
Results may differ from a plain program's by a relative error of at most 0.0005.
Values may be sent and summed in bfloat16 or wider, within the bound.
No kernel may reach another device: no remote copies, remote signals or barrier semaphores. Data moves between devices by JAX's collectives and lax.ppermute only.
A program may use at most 128 MiB of HBM per device.

v0:
```python
import jax
import jax.numpy as jnp
from jax import lax
from jax.experimental import pallas as pl
from jax.experimental.pallas import tpu as pltpu
from jax.sharding import Mesh, PartitionSpec as P

SCALE = 2.0**-7
HIGH = lax.Precision.HIGHEST
TILE = 128
SPAN = 8


def ring(count, shift):
    return [(i, (i + shift) % count) for i in range(count)]


def shifted(value, axis, count, shift):
    return lax.ppermute(value, axis, ring(count, shift))


def exchanged(value, axis):
    return lax.all_to_all(value, axis, 0, 0, tiled=True)


def after(value, *others):
    return lax.optimization_barrier((value,) + others)[0]


def copies(value, axis, count):
    return exchanged(jnp.broadcast_to(value[None], (count,) + value.shape), axis)


def gather_ring4(value, axis, *others):
    half = value.shape[0] // 2
    low = shifted(value, axis, 4, 1)
    high = shifted(value, axis, 4, -1)
    low, high = lax.optimization_barrier((low, high) + others)[:2]
    across = jnp.concatenate(
        [shifted(low[:half], axis, 4, 1), shifted(high[half:], axis, 4, -1)],
        axis=0,
    )
    return [value, low, across, high]


def gather_ring8(value, axis, gates):
    half = value.shape[0] // 2
    got = [value] + [None] * 7
    low = high = value
    for k in range(1, 4):
        low = shifted(low, axis, 8, 1)
        high = shifted(high, axis, 8, -1)
        low, high = lax.optimization_barrier((low, high) + gates.get(k, ()))[:2]
        got[k], got[8 - k] = low, high
    got[4] = jnp.concatenate(
        [shifted(low[:half], axis, 8, 1), shifted(high[half:], axis, 8, -1)],
        axis=0,
    )
    return got


def add_tiles(table, tiles, out):
    first = pl.program_id(0) * SPAN

    def one(source, carry):
        row = pl.multiple_of(table[1, source] * TILE, TILE)
        for t in range(2):
            at = table[2 + t, source] - first

            @pl.when((table[0, source] > 0) & (at >= 0) & (at < SPAN))
            def _():
                col = pl.multiple_of(at * TILE, TILE)
                out[pl.ds(row, TILE), pl.ds(col, TILE)] += tiles[
                    source, :, t * TILE : (t + 1) * TILE
                ]

        return carry

    lax.fori_loop(0, tiles.shape[0], one, 0)


def first_kernel(table, place, weight, near, far, diag, tiles, out):

    def product(q, carry):
        span = pl.ds(pl.multiple_of(q * 2 * TILE, 2 * TILE), 2 * TILE)
        out[:, span] = -lax.dot_general(
            weight[...],
            jnp.concatenate([near[:, span], far[:, span]], axis=0),
            (((0,), (0,)), ((), ())),
            precision=HIGH,
            preferred_element_type=jnp.float32,
        )
        return carry

    lax.fori_loop(0, SPAN // 2, product, 0)
    same = lax.broadcasted_iota(jnp.int32, (TILE, TILE), 0) == lax.broadcasted_iota(
        jnp.int32, (TILE, TILE), 1
    )
    for i in range(2):
        at = place[0] + i - pl.program_id(0) * SPAN

        @pl.when((at >= 0) & (at < SPAN))
        def _():
            col = pl.multiple_of(at * TILE, TILE)
            out[i * TILE : (i + 1) * TILE, pl.ds(col, TILE)] += jnp.where(
                same, diag[i : i + 1, :], 0.0
            )

    add_tiles(table, tiles, out)


def second_kernel(table, start, tiles, out):
    out[...] = start[...]
    add_tiles(table, tiles, out)


def factor_kernel(matrix, upper, inverse, work):
    size = matrix.shape[0]
    work[...] = matrix[...]
    down = lax.broadcasted_iota(jnp.int32, (size, size), 0)
    along = lax.broadcasted_iota(jnp.int32, (size, size), 1)
    inverse[...] = jnp.where(down == along, 1.0, 0.0)
    place = lax.broadcasted_iota(jnp.int32, (1, size), 1)
    depth = lax.broadcasted_iota(jnp.int32, (size, 1), 0)

    def step(j, carry):
        row = work[pl.ds(j, 1), :]
        pivot = jnp.sum(jnp.where(place == j, row, 0.0), axis=1, keepdims=True)
        scale = 1.0 / jnp.sqrt(pivot)
        row = jnp.where(place >= j, row * scale, 0.0)
        column = jnp.sum(jnp.where(along == j, work[...], 0.0), axis=1, keepdims=True)
        column = jnp.where(depth > j, column * scale, 0.0)
        solved = inverse[pl.ds(j, 1), :] * scale
        work[...] -= column * row
        inverse[...] -= column * solved
        inverse[pl.ds(j, 1), :] = solved
        upper[pl.ds(j, 1), :] = row
        return carry

    lax.fori_loop(0, size, step, 0)


def factored(matrix):
    shape = jax.ShapeDtypeStruct(matrix.shape, jnp.float32)
    return pl.pallas_call(
        factor_kernel,
        out_shape=(shape, shape),
        scratch_shapes=[pltpu.VMEM(matrix.shape, jnp.float32)],
        name="factored",
    )(matrix)


def whole(value):
    return pl.BlockSpec(value.shape, lambda i, *_: (0,) * len(value.shape), pipeline_mode=pl.Buffered(1))


def columns(rows):
    return pl.BlockSpec((rows, SPAN * TILE), lambda i, *_: (0, i))


def first_sum(table, place, weight, near, far, diag, tiles, shape):
    return pl.pallas_call(
        first_kernel,
        grid_spec=pltpu.PrefetchScalarGridSpec(
            num_scalar_prefetch=2,
            grid=(shape[1] // (SPAN * TILE),),
            in_specs=[
                whole(weight),
                columns(near.shape[0]),
                columns(far.shape[0]),
                whole(diag),
                whole(tiles),
            ],
            out_specs=columns(shape[0]),
        ),
        out_shape=jax.ShapeDtypeStruct(shape, jnp.float32),
        name="first_sum",
    )(table, place, weight, near, far, diag, tiles)


def second_sum(table, start, tiles):
    return pl.pallas_call(
        second_kernel,
        grid_spec=pltpu.PrefetchScalarGridSpec(
            num_scalar_prefetch=1,
            grid=(start.shape[1] // (SPAN * TILE),),
            in_specs=[columns(start.shape[0]), whole(tiles)],
            out_specs=columns(start.shape[0]),
        ),
        out_shape=jax.ShapeDtypeStruct(start.shape, jnp.float32),
        name="second_sum",
    )(table, start, tiles)


def per_device(factor_inv, coupling, first_diag, pattern):
    ny, nz, nc, nx = 4, 8, 2, 4
    yi, zi, ci, xi = (lax.axis_index(a) for a in ("y", "z", "c", "x"))
    count = ny * nz * nc
    here = (yi * nz + zi) * nc + ci
    per_range = 32
    f32 = jnp.float32

    def slabs_of(s):
        return jnp.dot(factor_inv[s], coupling[s], preferred_element_type=f32).astype(jnp.bfloat16)

    slab0 = slabs_of(0)
    slab1 = slabs_of(1)
    block0 = gather_ring4(slab0, "x", slab1)

    def product(block, slab):
        return jnp.einsum("nr,nc->rc", block, slab, preferred_element_type=f32)

    block1 = gather_ring4(after(slab1, block0[2]), "x")

    lead = jnp.where(
        xi == 0, block0[0], jnp.where(xi == 1, block0[1], jnp.where(xi == 2, block0[2], block0[3]))
    )[:, :TILE]
    corner = product(lead, lead)
    unit = jnp.eye(TILE, dtype=f32)
    corner = corner + jnp.where(here == 0, 1.0, 0.0) * (first_diag[0][:, None] * unit)
    top = jnp.concatenate([product(lead, slab0), corner], axis=1).reshape(count, 6, TILE)
    said = jnp.pad(pattern.reshape(1, 1, -1).astype(f32), ((0, 0), (0, 1), (0, TILE - 16)))
    top = jnp.concatenate([top, jnp.broadcast_to(said, (count, 2, TILE))], axis=1)
    top = top.reshape(ny, nz, nc, 8, TILE).transpose(0, 2, 1, 3, 4)
    top = exchanged(top.reshape(ny * nc, nz, 8, TILE), ("y", "c"))
    top = exchanged(top.transpose(1, 0, 2, 3), "z")
    top = top.reshape(count, 8, TILE)
    names = top[:, 6, :16]
    entry = jnp.arange(16, dtype=jnp.int32)[None, :]
    firsts = [
        jnp.sum(jnp.where(entry == xi * 2 + t, names, 0.0), axis=1) - xi * per_range for t in range(2)
    ]
    firsts = jnp.stack(firsts, axis=1).reshape(-1)
    pick = (jnp.arange(per_range, dtype=f32)[:, None] == firsts[None, :]).astype(f32)
    parts = top[:, :6].reshape(count, 2, 3, TILE)
    tiles = parts[:, :, :2].transpose(0, 2, 1, 3).reshape(count * 2, 2 * TILE)
    rows = jnp.dot(pick, tiles, precision=HIGH, preferred_element_type=f32)
    rows = rows.reshape(per_range, 2, TILE).transpose(1, 0, 2).reshape(2, per_range * TILE)
    summed = jnp.sum(parts[:, :, 2], axis=0)
    rows = jnp.concatenate(
        [jnp.where(xi == 0, summed, rows[:, :TILE]), rows[:, TILE:], summed], axis=1
    )
    rows = copies(rows, "z", nz).reshape(2 * nz, -1)

    made = jnp.stack(
        [
            jnp.stack([product(b[-j % nx], slab) for b, slab in ((block0, slab0), (block1, slab1))])
            for j in range(nx)
        ]
    )
    made = (made * SCALE).astype(jnp.float16).reshape(nx, 2, 2, TILE, 2 * TILE)
    made = jnp.stack(
        [
            lax.dynamic_index_in_dim(made, lax.rem(r - xi + nx, nx), 0, keepdims=False)
            for r in range(ny)
        ]
    )
    picked = exchanged(made, "y")

    near = copies(after(rows, picked), "y", ny).reshape(count, -1)
    far = shifted(near, "c", nc, 1)

    def in_order(value):
        value = value.reshape(nc, ny * nz, 2, -1)
        value = jnp.where(ci == 0, value, value[::-1])
        return value.transpose(1, 0, 2, 3).reshape(TILE, -1)

    def as_lies(value):
        value = value.reshape(ny * nz, nc, 2, -1).transpose(1, 0, 2, 3)
        value = jnp.where(ci == 0, value, value[::-1])
        return value.reshape(TILE, -1)

    edge = per_range * TILE
    own = lax.dynamic_slice_in_dim(near, lax.rem(here - ci, 16) * 2 * TILE, 4 * TILE, 1)
    own = lax.dynamic_index_in_dim(copies(own, "x", nx), yi, 0, keepdims=False)
    own, others = (own[:, : 2 * TILE], own[:, 2 * TILE :])
    own, others = jnp.where(ci == 0, own, others), jnp.where(ci == 0, others, own)
    own = jnp.concatenate([own, shifted(others, "c", nc, 1)], axis=0)
    bulk = gather_ring8(picked, "z", {2: (far,)})
    corner = in_order(jnp.concatenate([near[:, edge:], far[:, edge:]], axis=0))
    upper, inverse = factored(after(corner, bulk[1], bulk[7]))
    solved = jnp.dot(inverse, in_order(own), precision=HIGH, preferred_element_type=f32)
    solved = jnp.concatenate(
        [jnp.where(here == 0, upper, solved[:, :TILE]), solved[:, TILE:]], axis=1
    )
    panel = solved.T
    weight = as_lies(jnp.dot(inverse.T, solved, precision=HIGH, preferred_element_type=f32))

    names = names.reshape(nz, ny * nc * 16)
    names = jnp.take(names, lax.rem(zi - jnp.arange(nz) + nz, nz), axis=0).reshape(count, 16)
    in_range = entry % 8 // 2 == yi
    owner = jnp.floor(names * 0.5)
    first_half = entry < 8

    def scattered(owned):
        match = in_range & (owner == owned)
        hits = [
            jnp.sum(jnp.where(match & half, 1.0, 0.0), axis=1, keepdims=True)
            for half in (first_half, ~first_half)
        ]
        return match, hits

    match, hits = scattered(here.astype(f32))
    hit = jnp.where(first_half, hits[0], hits[1])
    fields = [
        (hits[0] + hits[1])[:, 0],
        jnp.sum(jnp.where(match, names - 2.0 * owner, 0.0), axis=1),
        jnp.sum(jnp.where(entry % 8 == xi * 2, hit * (names - xi * per_range), 0.0), axis=1),
        jnp.sum(jnp.where(entry % 8 == xi * 2 + 1, hit * (names - xi * per_range), 0.0), axis=1),
    ]
    fields = jnp.stack(fields).astype(jnp.int32).reshape(4, nz, ny, nc).transpose(0, 3, 1, 2)
    fields = jnp.where(ci == 0, fields, fields[:, ::-1])

    def flags(match):
        match = match.reshape(nz, ny, nc, 2, 8)
        match = lax.dynamic_index_in_dim(match, ci, 2, keepdims=False)
        return lax.dynamic_slice_in_dim(match, yi * 2, 2, 3).transpose(2, 3, 0, 1)

    to_me = flags(match)
    to_other = flags(scattered((here + 1 - 2 * ci).astype(f32))[0])

    def choose(k, match):
        def flag(s, t):
            return match[s, t, k][:, None, None]

        got = bulk[k]
        second = jnp.where(flag(1, 0), got[:, 1, 0], got[:, 1, 1])
        return jnp.where(flag(0, 0), got[:, 0, 0], jnp.where(flag(0, 1), got[:, 0, 1], second))

    def batch(ks):
        mine = jnp.concatenate([choose(k, to_me) for k in ks], axis=0)
        other = jnp.concatenate([choose(k, to_other) for k in ks], axis=0)
        both = jnp.concatenate([mine, shifted(other, "c", nc, 1)], axis=0)
        table = jnp.concatenate([fields[:, :, k] for k in ks], axis=2)
        return table.reshape(4, -1), both.astype(f32) * (1.0 / SCALE)

    first_table, first_tiles = batch((0, 1, 7, 2, 6))
    place = (here * 2 - xi * per_range).astype(jnp.int32)[None]
    weight = after(weight, bulk[3], bulk[5])
    shape = (2 * TILE, per_range * TILE)
    start = first_sum(first_table, place, weight, near, far, first_diag, first_tiles, shape)
    late = [batch((3, 5))]
    bulk[4] = after(bulk[4], start)
    late.append(batch((4,)))
    last_table = jnp.concatenate([e[0] for e in late], axis=1)
    last_tiles = jnp.concatenate([e[1] for e in late], axis=0)
    return panel, second_sum(last_table, start, last_tiles)


def solution(mesh):
    grid = Mesh(mesh.devices.reshape(4, 8, 2, 4), ("y", "z", "c", "x"))
    scen = ("y", "z", "c")
    in_specs = (P(scen, None, None), P(scen, None, "x"), P(scen, None), P(scen, None))
    out_specs = (P(scen, None), P(scen, "x"))

    return jax.shard_map(
        per_device, mesh=grid, in_specs=in_specs, out_specs=out_specs, check_vma=False
    )
```

profile of v0, /device:TPU:1, one launch (start us, length us, event | category | flops | bytes accessed | tf_op | source)
XLA Modules:
  0.0 225.1 jit_solution(13985956787742426929)
XLA Ops:
  0.7 2.5 %fusion.7 = bf16[1024,256]{1,0:T(8,128)(2,1)S(1)} fusion(bf16[2,1024,1024]{2,1,0:T(8,128)(2,1)} %param.4, bf16[2,1024,256]{2,1,0:T(8,128)(2,1)} %param.5), kind=kOutput, calls=%fused_computation.12 | convolution fusion | flops 537133056 | bytes 3145728 | tf_op jit(solution)/shard_map/dot_general | solution.py:204
  3.1 2.1 collective-permute-start
  7.5 2.3 %fusion.10 = bf16[1024,256]{1,0:T(8,128)(2,1)S(1)} fusion(bf16[2,1024,1024]{2,1,0:T(8,128)(2,1)} %param.4, bf16[2,1024,256]{2,1,0:T(8,128)(2,1)S(1)} %copy-done.11), kind=kOutput, calls=%fused_computation.13 | convolution fusion | flops 537133056 | bytes 3145728 | tf_op jit(solution)/shard_map/dot_general | solution.py:204
  9.8 6.2 %collective-permute-done = bf16[1024,256]{1,0:T(8,128)(2,1)S(1)} collective-permute-done((bf16[1024,256]{1,0:T(8,128)(2,1)S(1)}, bf16[1024,256]{1,0:T(8,128)(2,1)S(1)}, u32[]{:S(2)}, u32[]{:S(2)}) %collective-permute-start) | collective-permute-done | bytes 524320 | tf_op jit(solution)/shard_map/ppermute | solution.py:19
  22.4 2.1 collective-permute-done.2
  26.7 2.1 collective-permute-start.5
  30.3 8.1 %all-to-all-start = ((f32[8,8,8,128]{3,2,1,0:T(8,128)}), f32[8,8,8,128]{3,2,1,0:T(8,128)S(1)}, u32[]{:S(2)}, u32[]{:S(2)}) async-start(f32[8,8,8,128]{3,2,1,0:T(8,128)} %bitcast.7), calls=%async_computation | async-start | bytes 524288 | tf_op jit(solution)/shard_map/all_to_all | solution.py:23
  39.1 5.8 %all-to-all-done = f32[8,8,8,128]{3,2,1,0:T(8,128)S(1)} async-done(((f32[8,8,8,128]{3,2,1,0:T(8,128)}), f32[8,8,8,128]{3,2,1,0:T(8,128)S(1)}, u32[]{:S(2)}, u32[]{:S(2)}) %all-to-all-start) | async-done | bytes 262176 | tf_op jit(solution)/shard_map/all_to_all | solution.py:23
  45.6 8.2 %all-to-all-start.1 = ((f32[8,8,8,128]{3,2,1,0:T(8,128)}), f32[8,8,8,128]{3,2,1,0:T(8,128)S(1)}, u32[]{:S(2)}, u32[]{:S(2)}) async-start(f32[8,8,8,128]{3,2,1,0:T(8,128)} %copy.101), calls=%async_computation.1 | async-start | bytes 524288 | tf_op jit(solution)/shard_map/all_to_all | solution.py:23
  59.6 4.4 %all-to-all-done.1 = f32[8,8,8,128]{3,2,1,0:T(8,128)S(1)} async-done(((f32[8,8,8,128]{3,2,1,0:T(8,128)}), f32[8,8,8,128]{3,2,1,0:T(8,128)S(1)}, u32[]{:S(2)}, u32[]{:S(2)}) %all-to-all-start.1) | async-done | bytes 262176 | tf_op jit(solution)/shard_map/all_to_all | solution.py:23
  65.8 3.6 %all-to-all-start.2 = ((f32[8,2,4224]{2,1,0:T(2,128)}), f32[8,2,4224]{2,1,0:T(2,128)S(1)}, u32[]{:S(2)}, u32[]{:S(2)}) async-start(f32[8,2,4224]{2,1,0:T(2,128)} %broadcast_in_dim.456), calls=%async_computation.2 | async-start | bytes 540672 | tf_op jit(solution)/shard_map/all_to_all | solution.py:23
  73.4 5.2 %all-to-all-done.2 = f32[8,2,4224]{2,1,0:T(2,128)S(1)} async-done(((f32[8,2,4224]{2,1,0:T(2,128)}), f32[8,2,4224]{2,1,0:T(2,128)S(1)}, u32[]{:S(2)}, u32[]{:S(2)}) %all-to-all-start.2) | async-done | bytes 270368 | tf_op jit(solution)/shard_map/all_to_all | solution.py:23
  78.7 3.5 %all-to-all-start.3 = ((f16[4,2,2,128,256]{4,3,2,1,0:T(8,128)(2,1)}), f16[4,2,2,128,256]{4,3,2,1,0:T(8,128)(2,1)S(1)}, u32[]{:S(2)}, u32[]{:S(2)}) async-start(f16[4,2,2,128,256]{4,3,2,1,0:T(8,128)(2,1)} %pad_maximum_fusion.1), calls=%async_computation.3 | async-start | bytes 2097152 | tf_op jit(solution)/shard_map/all_to_all | solution.py:23
  86.4 7.0 %all-to-all-done.3 = f16[4,2,2,128,256]{4,3,2,1,0:T(8,128)(2,1)S(1)} async-done(((f16[4,2,2,128,256]{4,3,2,1,0:T(8,128)(2,1)}), f16[4,2,2,128,256]{4,3,2,1,0:T(8,128)(2,1)S(1)}, u32[]{:S(2)}, u32[]{:S(2)}) %all-to-all-start.3) | async-done | bytes 1048608 | tf_op jit(solution)/shard_map/all_to_all | solution.py:23
  94.4 3.5 %all-to-all-start.4 = ((f32[4,16,4224]{2,1,0:T(8,128)}), f32[4,16,4224]{2,1,0:T(8,128)S(1)}, u32[]{:S(2)}, u32[]{:S(2)}) async-start(f32[4,16,4224]{2,1,0:T(8,128)} %broadcast_in_dim.457), calls=%async_computation.4 | async-start | bytes 2162688 | tf_op jit(solution)/shard_map/all_to_all | solution.py:23
  99.3 2.5 %collective-permute-start.10 = (f16[4,2,2,128,256]{4,3,0,2,1:T(8,128)(2,1)}, f16[4,2,2,128,256]{4,3,0,2,1:T(8,128)(2,1)}, u32[]{:S(2)}, u32[]{:S(2)}) collective-permute-start(f16[4,2,2,128,256]{4,3,0,2,1:T(8,128)(2,1)} %copy.107), channel_id=1, source_target_pairs={{0,56},{8,0},{16,8},{24,16},{32,24},{40,32},{48,40},{56,48},{1,57}... | collective-permute-start | bytes 3145736 | tf_op jit(solution)/shard_map/ppermute | solution.py:19
  105.0 3.3 %all-to-all-done.4 = f32[4,16,4224]{2,1,0:T(8,128)S(1)} async-done(((f32[4,16,4224]{2,1,0:T(8,128)}), f32[4,16,4224]{2,1,0:T(8,128)S(1)}, u32[]{:S(2)}, u32[]{:S(2)}) %all-to-all-start.4) | async-done | bytes 1081376 | tf_op jit(solution)/shard_map/all_to_all | solution.py:23
  109.2 4.2 %all-to-all-start.5 = ((f32[4,64,512]{2,1,0:T(8,128)}), f32[4,64,512]{2,1,0:T(8,128)}, u32[]{:S(2)}, u32[]{:S(2)}) async-start(f32[4,64,512]{2,1,0:T(8,128)} %broadcast_in_dim.458), calls=%async_computation.5 | async-start | bytes 1048576 | tf_op jit(solution)/shard_map/all_to_all | solution.py:23
  114.6 6.0 %collective-permute-start.8 = (f32[64,4224]{1,0:T(8,128)S(1)}, f32[64,4224]{1,0:T(8,128)S(1)}, u32[]{:S(2)}, u32[]{:S(2)}) collective-permute-start(f32[64,4224]{1,0:T(8,128)S(1)} %bitcast.291), channel_id=1, source_target_pairs={{0,4},{4,0},{1,5},{5,1},{2,6},{6,2},{3,7},{7,3},{8,12},{12,8},{9,1... | collective-permute-start | bytes 3244040 | tf_op jit(solution)/shard_map/ppermute | solution.py:19
  120.8 2.5 %collective-permute-start.13 = (f16[4,2,2,128,256]{4,3,0,2,1:T(8,128)(2,1)}, f16[4,2,2,128,256]{4,3,0,2,1:T(8,128)(2,1)}, u32[]{:S(2)}, u32[]{:S(2)}) collective-permute-start(f16[4,2,2,128,256]{4,3,0,2,1:T(8,128)(2,1)} %collective-permute-done.10), channel_id=1, source_target_pairs={{0,56},{8,0},{16,8},{24,16},{32,24},{40,32},{48,40},{56,48},{1,57}... | collective-permute-start | bytes 3145736 | tf_op jit(solution)/shard_map/ppermute | solution.py:19
  123.4 2.5 %fusion.56 = (f16[20,128,256]{2,1,0:T(8,128)(2,1)}, f16[40,128,256]{2,1,0:T(8,128)(2,1)}) fusion(f16[20,128,256]{2,1,0:T(8,128)(2,1)} %get-tuple-element.126, pred[4]{0:T(512)(128)(4,1)S(1)} %get-tuple-element.100, pred[4]{0:T(512)(128)(4,1)S(1)} %get-tuple-element.102, pred[4]{0:T(512)(128)(4,1)S(1)} %get-tuple-element.101, ...), kind=kLoop, calls=%fused_computation.85 | loop fusion | flops 786432 | bytes 1572888
  126.8 7.2 %collective-permute-start.11 = (f32[64,256]{1,0:T(8,128)S(1)}, f32[64,256]{1,0:T(8,128)S(1)}, u32[]{:S(2)}, u32[]{:S(2)}) collective-permute-start(f32[64,256]{1,0:T(8,128)S(1)} %get-tuple-element.137), channel_id=1, source_target_pairs={{0,4},{4,0},{1,5},{5,1},{2,6},{6,2},{3,7},{7,3},{8,12},{12,8},{9,1... | collective-permute-start | bytes 196616 | tf_op jit(solution)/shard_map/ppermute | solution.py:19
  134.1 2.5 %fusion.50 = (f16[20,128,256]{2,1,0:T(8,128)(2,1)}, f16[40,128,256]{2,1,0:T(8,128)(2,1)}) fusion(f16[20,128,256]{2,1,0:T(8,128)(2,1)} %get-tuple-element.124, pred[4]{0:T(512)(128)(4,1)S(1)} %get-tuple-element.97, pred[4]{0:T(512)(128)(4,1)S(1)} %get-tuple-element.98, pred[4]{0:T(512)(128)(4,1)S(1)} %get-tuple-element.99, ...), kind=kLoop, calls=%fused_computation.77 | loop fusion | flops 786432 | bytes 1572888
  137.7 15.7 %factored.1 = (f32[128,128]{1,0:T(8,128)}, f32[128,128]{1,0:T(8,128)}) custom-call(f32[128,128]{1,0:T(8,128)} %bitcast.311), custom_call_target="tpu_custom_call" | custom-call | tf_op jit(solution)/shard_map/factored/pallas_call | solution.py:145
  153.5 2.7 %collective-permute-start.15 = (f16[4,2,2,128,256]{4,3,0,2,1:T(8,128)(2,1)}, f16[4,2,2,128,256]{4,3,0,2,1:T(8,128)(2,1)S(1)}, u32[]{:S(2)}, u32[]{:S(2)}) collective-permute-start(f16[4,2,2,128,256]{4,3,0,2,1:T(8,128)(2,1)} %collective-permute-done.13), channel_id=1, source_target_pairs={{0,56},{8,0},{16,8},{24,16},{32,24},{40,32},{48,40},{56,48},{1,57}... | collective-permute-start | bytes 3145736 | tf_op jit(solution)/shard_map/ppermute | solution.py:19
  156.2 2.5 %fusion.44 = (f16[20,128,256]{2,1,0:T(8,128)(2,1)}, f16[40,128,256]{2,1,0:T(8,128)(2,1)}) fusion(f16[20,128,256]{2,1,0:T(8,128)(2,1)} %get-tuple-element.122, pred[4]{0:T(512)(128)(4,1)} %get-tuple-element.94, pred[4]{0:T(512)(128)(4,1)} %get-tuple-element.95, pred[4]{0:T(512)(128)(4,1)} %get-tuple-element.96, ...), kind=kLoop, calls=%fused_computation.69 | loop fusion | flops 786432 | bytes 1575936
  158.7 2.5 %fusion.38 = (f16[20,128,256]{2,1,0:T(8,128)(2,1)}, f16[40,128,256]{2,1,0:T(8,128)(2,1)}) fusion(f16[20,128,256]{2,1,0:T(8,128)(2,1)} %get-tuple-element.120, pred[4]{0:T(512)(128)(4,1)} %get-tuple-element.91, pred[4]{0:T(512)(128)(4,1)} %get-tuple-element.92, pred[4]{0:T(512)(128)(4,1)} %get-tuple-element.93, ...), kind=kLoop, calls=%fused_computation.61 | loop fusion | flops 786432 | bytes 1575936 | tf_op jit(solution)/shard_map/concatenate | solution.py:332
  168.0 11.6 %collective-permute-done.14 = f16[4,2,2,128,256]{4,3,0,2,1:T(8,128)(2,1)S(1)} collective-permute-done((f16[4,2,2,128,256]{4,3,0,2,1:T(8,128)(2,1)}, f16[4,2,2,128,256]{4,3,0,2,1:T(8,128)(2,1)S(1)}, u32[]{:S(2)}, u32[]{:S(2)}) %collective-permute-start.14) | collective-permute-done | bytes 1048608 | tf_op jit(solution)/shard_map/ppermute | solution.py:19
  181.5 2.4 %collective-permute-start.19 = (f16[2,2,2,128,256]{4,3,0,2,1:T(8,128)(2,1)}, f16[2,2,2,128,256]{4,3,0,2,1:T(8,128)(2,1)}, u32[]{:S(2)}, u32[]{:S(2)}) collective-permute-start(f16[2,2,2,128,256]{4,3,0,2,1:T(8,128)(2,1)} %slice.470), channel_id=1, source_target_pairs={{0,56},{8,0},{16,8},{24,16},{32,24},{40,32},{48,40},{56,48},{1,57}... | collective-permute-start | bytes 1572872 | tf_op jit(solution)/shard_map/ppermute | solution.py:19
  190.1 4.7 %convert_multiply_fusion.tiles = f32[40,128,256]{2,1,0:T(8,128)} fusion(f16[40,128,256]{2,1,0:T(8,128)(2,1)} %constant_dynamic-update-slice_fusion.2), kind=kLoop, calls=%fused_computation.1 | loop fusion | flops 2621440 | bytes 7864320 | tf_op jit(solution)/shard_map/mul | solution.py:335
  194.7 16.1 %first_sum.1.start = f32[256,4096]{1,0:T(8,128)} custom-call(s32[4,40]{1,0:T(4,128)} %reshape.355.table, s32[1]{0:T(128)} %bitcast.36.place, f32[128,256]{1,0:T(8,128)} %reshape.357.weight, f32[64,4224]{1,0:T(8,128)} %bitcast.293, f32[64,4224]{1,0:T(8,128)} %copy-done.1, f32[2,128]{1,0:T(2,128)} %diag.1, f32[40,128,256]{2,1,0:T(8,128)} %convert_multiply_fusion.tiles), custom_call_target="tpu_custom_call" | custom-call | tf_op jit(solution)/shard_map/first_sum/pallas_call | solution.py:162
  217.1 8.0 %second_sum.1 = f32[256,4096]{1,0:T(8,128)} custom-call(s32[4,24]{1,0:T(4,128)} %pad_add_fusion.1.table, f32[256,4096]{1,0:T(8,128)} %first_sum.1.start, f32[24,128,256]{2,1,0:T(8,128)} %pad_maximum_fusion.tiles), custom_call_target="tpu_custom_call" | custom-call | tf_op jit(solution)/shard_map/second_sum/pallas_call | solution.py:182
  (184 shorter events, 60.2 us)
Async XLA Ops:
  3.1 12.8 %collective-permute-start = (bf16[1024,256]{1,0:T(8,128)(2,1)S(1)}, bf16[1024,256]{1,0:T(8,128)(2,1)S(1)}, u32[]{:S(2)}, u32[]{:S(2)}) collective-permute-start(bf16[1024,256]{1,0:T(8,128)(2,1)S(1)} %fusion.7), channel_id=1, source_target_pairs={{0,1},{1,2},{2,3},{3,0},{4,5},{5,6},{6,7},{7,4},{8,9},{9,10},{10,1... | collective-permute-start | bytes 1572872 | tf_op jit(solution)/shard_map/ppermute | solution.py:19
  5.2 12.2 %collective-permute-start.1 = (bf16[1024,256]{1,0:T(8,128)(2,1)S(1)}, bf16[1024,256]{1,0:T(8,128)(2,1)S(1)}, u32[]{:S(2)}, u32[]{:S(2)}) collective-permute-start(bf16[1024,256]{1,0:T(8,128)(2,1)S(1)} %fusion.7), channel_id=1, source_target_pairs={{0,3},{1,0},{2,1},{3,2},{4,7},{5,4},{6,5},{7,6},{8,11},{9,8},{10,9... | collective-permute-start | bytes 1572872 | tf_op jit(solution)/shard_map/ppermute | solution.py:19
  17.5 7.0 %collective-permute-start.2 = (bf16[512,256]{1,0:T(8,128)(2,1)S(1)}, bf16[512,256]{1,0:T(8,128)(2,1)S(1)}, u32[]{:S(2)}, u32[]{:S(2)}) collective-permute-start(bf16[512,256]{1,0:T(8,128)(2,1)S(1)} %slice.372), channel_id=1, source_target_pairs={{0,1},{1,2},{2,3},{3,0},{4,5},{5,6},{6,7},{7,4},{8,9},{9,10},{10,1... | collective-permute-start | bytes 786440 | tf_op jit(solution)/shard_map/ppermute | solution.py:19
  20.1 5.8 %collective-permute-start.3 = (bf16[512,256]{1,0:T(8,128)(2,1)S(1)}, bf16[512,256]{1,0:T(8,128)(2,1)S(1)}, u32[]{:S(2)}, u32[]{:S(2)}) collective-permute-start(bf16[512,256]{1,0:T(8,128)(2,1)S(1)} %slice.373), channel_id=1, source_target_pairs={{0,3},{1,0},{2,1},{3,2},{4,7},{5,4},{6,5},{7,6},{8,11},{9,8},{10,9... | collective-permute-start | bytes 786440 | tf_op jit(solution)/shard_map/ppermute | solution.py:19
  26.0 27.8 %collective-permute-start.4 = (bf16[1024,256]{1,0:T(8,128)(2,1)S(1)}, bf16[1024,256]{1,0:T(8,128)(2,1)S(1)}, u32[]{:S(2)}, u32[]{:S(2)}) collective-permute-start(bf16[1024,256]{1,0:T(8,128)(2,1)S(1)} %fusion.10), channel_id=1, source_target_pairs={{0,1},{1,2},{2,3},{3,0},{4,5},{5,6},{6,7},{7,4},{8,9},{9,10},{10,1... | collective-permute-start | bytes 1572872 | tf_op jit(solution)/shard_map/ppermute | solution.py:19
  26.7 27.1 %collective-permute-start.5 = (bf16[1024,256]{1,0:T(8,128)(2,1)S(1)}, bf16[1024,256]{1,0:T(8,128)(2,1)}, u32[]{:S(2)}, u32[]{:S(2)}) collective-permute-start(bf16[1024,256]{1,0:T(8,128)(2,1)S(1)} %fusion.10), channel_id=1, source_target_pairs={{0,3},{1,0},{2,1},{3,2},{4,7},{5,4},{6,5},{7,6},{8,11},{9,8},{10,9... | collective-permute-start | bytes 1572872 | tf_op jit(solution)/shard_map/ppermute | solution.py:19
  30.3 14.6 %all-to-all-start = ((f32[8,8,8,128]{3,2,1,0:T(8,128)}), f32[8,8,8,128]{3,2,1,0:T(8,128)S(1)}, u32[]{:S(2)}, u32[]{:S(2)}) async-start(f32[8,8,8,128]{3,2,1,0:T(8,128)} %bitcast.7), calls=%async_computation | async-start | bytes 524288 | tf_op jit(solution)/shard_map/all_to_all | solution.py:23
  45.6 18.4 %all-to-all-start.1 = ((f32[8,8,8,128]{3,2,1,0:T(8,128)}), f32[8,8,8,128]{3,2,1,0:T(8,128)S(1)}, u32[]{:S(2)}, u32[]{:S(2)}) async-start(f32[8,8,8,128]{3,2,1,0:T(8,128)} %copy.101), calls=%async_computation.1 | async-start | bytes 524288 | tf_op jit(solution)/shard_map/all_to_all | solution.py:23
  55.4 14.7 %collective-permute-start.7 = (bf16[512,256]{1,0:T(8,128)(2,1)}, bf16[512,256]{1,0:T(8,128)(2,1)}, u32[]{:S(2)}, u32[]{:S(2)}) collective-permute-start(bf16[512,256]{1,0:T(8,128)(2,1)} %slice.383), channel_id=1, source_target_pairs={{0,3},{1,0},{2,1},{3,2},{4,7},{5,4},{6,5},{7,6},{8,11},{9,8},{10,9... | collective-permute-start | bytes 786440 | tf_op jit(solution)/shard_map/ppermute | solution.py:19
  57.8 12.3 %collective-permute-start.6 = (bf16[512,256]{1,0:T(8,128)(2,1)}, bf16[512,256]{1,0:T(8,128)(2,1)}, u32[]{:S(2)}, u32[]{:S(2)}) collective-permute-start(bf16[512,256]{1,0:T(8,128)(2,1)} %slice.382), channel_id=1, source_target_pairs={{0,1},{1,2},{2,3},{3,0},{4,5},{5,6},{6,7},{7,4},{8,9},{9,10},{10,1... | collective-permute-start | bytes 786440 | tf_op jit(solution)/shard_map/ppermute | solution.py:19
  64.0 7.5 %copy-start.2 = (f32[256,256]{1,0:T(8,128)S(1)}, f32[256,256]{1,0:T(8,128)}, u32[]{:S(2)}) copy-start(f32[256,256]{1,0:T(8,128)} %fusion.84) | copy-start | bytes 786436
  65.8 12.8 %all-to-all-start.2 = ((f32[8,2,4224]{2,1,0:T(2,128)}), f32[8,2,4224]{2,1,0:T(2,128)S(1)}, u32[]{:S(2)}, u32[]{:S(2)}) async-start(f32[8,2,4224]{2,1,0:T(2,128)} %broadcast_in_dim.456), calls=%async_computation.2 | async-start | bytes 540672 | tf_op jit(solution)/shard_map/all_to_all | solution.py:23
  78.7 14.7 %all-to-all-start.3 = ((f16[4,2,2,128,256]{4,3,2,1,0:T(8,128)(2,1)}), f16[4,2,2,128,256]{4,3,2,1,0:T(8,128)(2,1)S(1)}, u32[]{:S(2)}, u32[]{:S(2)}) async-start(f16[4,2,2,128,256]{4,3,2,1,0:T(8,128)(2,1)} %pad_maximum_fusion.1), calls=%async_computation.3 | async-start | bytes 2097152 | tf_op jit(solution)/shard_map/all_to_all | solution.py:23
  94.4 13.9 %all-to-all-start.4 = ((f32[4,16,4224]{2,1,0:T(8,128)}), f32[4,16,4224]{2,1,0:T(8,128)S(1)}, u32[]{:S(2)}, u32[]{:S(2)}) async-start(f32[4,16,4224]{2,1,0:T(8,128)} %broadcast_in_dim.457), calls=%async_computation.4 | async-start | bytes 2162688 | tf_op jit(solution)/shard_map/all_to_all | solution.py:23
  99.2 21.4 %collective-permute-start.9 = (f16[4,2,2,128,256]{4,3,0,2,1:T(8,128)(2,1)}, f16[4,2,2,128,256]{4,3,0,2,1:T(8,128)(2,1)}, u32[]{:S(2)}, u32[]{:S(2)}) collective-permute-start(f16[4,2,2,128,256]{4,3,0,2,1:T(8,128)(2,1)} %copy.107), channel_id=1, source_target_pairs={{0,8},{8,16},{16,24},{24,32},{32,40},{40,48},{48,56},{56,0},{1,9},... | collective-permute-start | bytes 3145736 | tf_op jit(solution)/shard_map/ppermute | solution.py:19
  99.3 21.3 %collective-permute-start.10 = (f16[4,2,2,128,256]{4,3,0,2,1:T(8,128)(2,1)}, f16[4,2,2,128,256]{4,3,0,2,1:T(8,128)(2,1)}, u32[]{:S(2)}, u32[]{:S(2)}) collective-permute-start(f16[4,2,2,128,256]{4,3,0,2,1:T(8,128)(2,1)} %copy.107), channel_id=1, source_target_pairs={{0,56},{8,0},{16,8},{24,16},{32,24},{40,32},{48,40},{56,48},{1,57}... | collective-permute-start | bytes 3145736 | tf_op jit(solution)/shard_map/ppermute | solution.py:19
  108.2 17.7 %copy-start = (f32[4,16,4224]{2,1,0:T(8,128)}, f32[4,16,4224]{2,1,0:T(8,128)S(1)}, u32[]{:S(2)}) copy-start(f32[4,16,4224]{2,1,0:T(8,128)S(1)} %all-to-all-done.4) | copy-start | bytes 3244036
  109.2 16.7 %all-to-all-start.5 = ((f32[4,64,512]{2,1,0:T(8,128)}), f32[4,64,512]{2,1,0:T(8,128)}, u32[]{:S(2)}, u32[]{:S(2)}) async-start(f32[4,64,512]{2,1,0:T(8,128)} %broadcast_in_dim.458), calls=%async_computation.5 | async-start | bytes 1048576 | tf_op jit(solution)/shard_map/all_to_all | solution.py:23
  114.6 22.3 %collective-permute-start.8 = (f32[64,4224]{1,0:T(8,128)S(1)}, f32[64,4224]{1,0:T(8,128)S(1)}, u32[]{:S(2)}, u32[]{:S(2)}) collective-permute-start(f32[64,4224]{1,0:T(8,128)S(1)} %bitcast.291), channel_id=1, source_target_pairs={{0,4},{4,0},{1,5},{5,1},{2,6},{6,2},{3,7},{7,3},{8,12},{12,8},{9,1... | collective-permute-start | bytes 3244040 | tf_op jit(solution)/shard_map/ppermute | solution.py:19
  120.6 32.8 %collective-permute-start.12 = (f16[4,2,2,128,256]{4,3,0,2,1:T(8,128)(2,1)}, f16[4,2,2,128,256]{4,3,0,2,1:T(8,128)(2,1)}, u32[]{:S(2)}, u32[]{:S(2)}) collective-permute-start(f16[4,2,2,128,256]{4,3,0,2,1:T(8,128)(2,1)} %collective-permute-done.9), channel_id=1, source_target_pairs={{0,8},{8,16},{16,24},{24,32},{32,40},{40,48},{48,56},{56,0},{1,9},... | collective-permute-start | bytes 3145736 | tf_op jit(solution)/shard_map/ppermute | solution.py:19
  120.8 32.6 %collective-permute-start.13 = (f16[4,2,2,128,256]{4,3,0,2,1:T(8,128)(2,1)}, f16[4,2,2,128,256]{4,3,0,2,1:T(8,128)(2,1)}, u32[]{:S(2)}, u32[]{:S(2)}) collective-permute-start(f16[4,2,2,128,256]{4,3,0,2,1:T(8,128)(2,1)} %collective-permute-done.10), channel_id=1, source_target_pairs={{0,56},{8,0},{16,8},{24,16},{32,24},{40,32},{48,40},{56,48},{1,57}... | collective-permute-start | bytes 3145736 | tf_op jit(solution)/shard_map/ppermute | solution.py:19
  126.8 9.8 %collective-permute-start.11 = (f32[64,256]{1,0:T(8,128)S(1)}, f32[64,256]{1,0:T(8,128)S(1)}, u32[]{:S(2)}, u32[]{:S(2)}) collective-permute-start(f32[64,256]{1,0:T(8,128)S(1)} %get-tuple-element.137), channel_id=1, source_target_pairs={{0,4},{4,0},{1,5},{5,1},{2,6},{6,2},{3,7},{7,3},{8,12},{12,8},{9,1... | collective-permute-start | bytes 196616 | tf_op jit(solution)/shard_map/ppermute | solution.py:19
  136.9 24.4 %copy-start.1 = (f32[64,4224]{1,0:T(8,128)}, f32[64,4224]{1,0:T(8,128)S(1)}, u32[]{:S(2)}) copy-start(f32[64,4224]{1,0:T(8,128)S(1)} %collective-permute-done.8.far) | copy-start | bytes 3244036
  153.4 8.5 %copy-start.5 = (f32[128,128]{1,0:T(8,128)S(1)}, f32[128,128]{1,0:T(8,128)}, u32[]{:S(2)}) copy-start(f32[128,128]{1,0:T(8,128)} %get-tuple-element.29) | copy-start | bytes 196612
  153.4 8.7 %copy-start.6 = (f32[128,128]{1,0:T(8,128)S(1)}, f32[128,128]{1,0:T(8,128)}, u32[]{:S(2)}) copy-start(f32[128,128]{1,0:T(8,128)} %get-tuple-element.28) | copy-start | bytes 196612
  153.4 26.2 %collective-permute-start.14 = (f16[4,2,2,128,256]{4,3,0,2,1:T(8,128)(2,1)}, f16[4,2,2,128,256]{4,3,0,2,1:T(8,128)(2,1)S(1)}, u32[]{:S(2)}, u32[]{:S(2)}) collective-permute-start(f16[4,2,2,128,256]{4,3,0,2,1:T(8,128)(2,1)} %collective-permute-done.12), channel_id=1, source_target_pairs={{0,8},{8,16},{16,24},{24,32},{32,40},{40,48},{48,56},{56,0},{1,9},... | collective-permute-start | bytes 3145736 | tf_op jit(solution)/shard_map/ppermute | solution.py:19
  153.5 26.1 %collective-permute-start.15 = (f16[4,2,2,128,256]{4,3,0,2,1:T(8,128)(2,1)}, f16[4,2,2,128,256]{4,3,0,2,1:T(8,128)(2,1)S(1)}, u32[]{:S(2)}, u32[]{:S(2)}) collective-permute-start(f16[4,2,2,128,256]{4,3,0,2,1:T(8,128)(2,1)} %collective-permute-done.13), channel_id=1, source_target_pairs={{0,56},{8,0},{16,8},{24,16},{32,24},{40,32},{48,40},{56,48},{1,57}... | collective-permute-start | bytes 3145736 | tf_op jit(solution)/shard_map/ppermute | solution.py:19
  161.3 27.4 %collective-permute-start.16 = (f16[20,128,256]{2,1,0:T(8,128)(2,1)}, f16[20,128,256]{2,1,0:T(8,128)(2,1)S(1)}, u32[]{:S(2)}, u32[]{:S(2)}) collective-permute-start(f16[20,128,256]{2,1,0:T(8,128)(2,1)} %get-tuple-element.118), channel_id=1, source_target_pairs={{0,4},{4,0},{1,5},{5,1},{2,6},{6,2},{3,7},{7,3},{8,12},{12,8},{9,1... | collective-permute-start | bytes 3932168 | tf_op jit(solution)/shard_map/ppermute | solution.py:19
  181.5 29.4 %collective-permute-start.19 = (f16[2,2,2,128,256]{4,3,0,2,1:T(8,128)(2,1)}, f16[2,2,2,128,256]{4,3,0,2,1:T(8,128)(2,1)}, u32[]{:S(2)}, u32[]{:S(2)}) collective-permute-start(f16[2,2,2,128,256]{4,3,0,2,1:T(8,128)(2,1)} %slice.470), channel_id=1, source_target_pairs={{0,56},{8,0},{16,8},{24,16},{32,24},{40,32},{48,40},{56,48},{1,57}... | collective-permute-start | bytes 1572872 | tf_op jit(solution)/shard_map/ppermute | solution.py:19
  183.9 27.0 %collective-permute-start.18 = (f16[2,2,2,128,256]{4,3,0,2,1:T(8,128)(2,1)}, f16[2,2,2,128,256]{4,3,0,2,1:T(8,128)(2,1)}, u32[]{:S(2)}, u32[]{:S(2)}) collective-permute-start(f16[2,2,2,128,256]{4,3,0,2,1:T(8,128)(2,1)} %slice.469), channel_id=1, source_target_pairs={{0,8},{8,16},{16,24},{24,32},{32,40},{40,48},{48,56},{56,0},{1,9},... | collective-permute-start | bytes 1572872 | tf_op jit(solution)/shard_map/ppermute | solution.py:19
  187.2 27.5 %collective-permute-start.17 = (f16[8,128,256]{2,1,0:T(8,128)(2,1)S(1)}, f16[8,128,256]{2,1,0:T(8,128)(2,1)S(1)}, u32[]{:S(2)}, u32[]{:S(2)}) collective-permute-start(f16[8,128,256]{2,1,0:T(8,128)(2,1)S(1)} %pad_maximum_fusion.3), channel_id=1, source_target_pairs={{0,4},{4,0},{1,5},{5,1},{2,6},{6,2},{3,7},{7,3},{8,12},{12,8},{9,1... | collective-permute-start | bytes 1572872 | tf_op jit(solution)/shard_map/ppermute | solution.py:19
  213.0 2.1 collective-permute-start.20
  (7 other events, 34.4 us)
where the time goes:
time: 226 us; the launch traced here: 225 us
  starting transfers between devices  68.6 us (30%)
  waiting for transfers between devices  48.5 us (21%)
  Pallas kernels  39.8 us (18%)
  other arithmetic  27.8 us (12%)
  local copies, waits for them, and re-layouts  26 us (12%)
  matrix products  12.9 us (6%)
    ppermute x21, starting transfers between devices, shifted(): return lax.ppermute(value, axis, ring(count, shift))  37.5 us
    all_to_all x6, starting transfers between devices, exchanged(): return lax.all_to_all(value, axis, 0, 0, tiled=True)  31.1 us
    all_to_all x6, waiting for transfers between devices, exchanged(): return lax.all_to_all(value, axis, 0, 0, tiled=True)  25.6 us
    ppermute x21, waiting for transfers between devices, shifted(): return lax.ppermute(value, axis, ring(count, shift))  22.9 us
    pallas_call x1, Pallas kernels, first_sum(): pl.pallas_call(first_kernel, grid_spec=pltpu.PrefetchScalarGridSpec(num_s...  16.1 us
    pallas_call x1, Pallas kernels, factored(): pl.pallas_call(factor_kernel, out_shape=(shape, shape), scratch_shapes=[p...  15.7 us
    unnamed x4, other arithmetic  8.81 us
    pallas_call x1, Pallas kernels, second_sum(): pl.pallas_call(second_kernel, grid_spec=pltpu.PrefetchScalarGridSpec(num_...  7.99 us
  transfers between devices with their start and end apart: 27, of which 11 were waited for; matrix products, arithmetic and copies ran while one was open for 27% of the time, Pallas kernels for 14%

commit v1 on v0

--- a/solution.py
+++ b/solution.py
@@ -43,22 +43,6 @@
     return [value, low, across, high]
 
 
-def gather_ring8(value, axis, gates):
-    half = value.shape[0] // 2
-    got = [value] + [None] * 7
-    low = high = value
-    for k in range(1, 4):
-        low = shifted(low, axis, 8, 1)
-        high = shifted(high, axis, 8, -1)
-        low, high = lax.optimization_barrier((low, high) + gates.get(k, ()))[:2]
-        got[k], got[8 - k] = low, high
-    got[4] = jnp.concatenate(
-        [shifted(low[:half], axis, 8, 1), shifted(high[half:], axis, 8, -1)],
-        axis=0,
-    )
-    return got
-
-
 def add_tiles(table, tiles, out):
     first = pl.program_id(0) * SPAN
 
@@ -82,17 +66,17 @@
 def first_kernel(table, place, weight, near, far, diag, tiles, out):
 
     def product(q, carry):
-        span = pl.ds(pl.multiple_of(q * 2 * TILE, 2 * TILE), 2 * TILE)
+        span = pl.ds(pl.multiple_of(q * 4 * TILE, 4 * TILE), 4 * TILE)
         out[:, span] = -lax.dot_general(
             weight[...],
             jnp.concatenate([near[:, span], far[:, span]], axis=0),
-            (((0,), (0,)), ((), ())),
+            (((1,), (0,)), ((), ())),
             precision=HIGH,
             preferred_element_type=jnp.float32,
         )
         return carry
 
-    lax.fori_loop(0, SPAN // 2, product, 0)
+    lax.fori_loop(0, SPAN // 4, product, 0)
     same = lax.broadcasted_iota(jnp.int32, (TILE, TILE), 0) == lax.broadcasted_iota(
         jnp.int32, (TILE, TILE), 1
     )
@@ -276,15 +260,17 @@
     own, others = (own[:, : 2 * TILE], own[:, 2 * TILE :])
     own, others = jnp.where(ci == 0, own, others), jnp.where(ci == 0, others, own)
     own = jnp.concatenate([own, shifted(others, "c", nc, 1)], axis=0)
-    bulk = gather_ring8(picked, "z", {2: (far,)})
+
+    def hop(low, high):
+        return shifted(low, "z", nz, 1), shifted(high, "z", nz, -1)
+
+    low1, high1 = hop(picked, picked)
+    low2, high2 = hop(low1, high1)
     corner = in_order(jnp.concatenate([near[:, edge:], far[:, edge:]], axis=0))
-    upper, inverse = factored(after(corner, bulk[1], bulk[7]))
-    solved = jnp.dot(inverse, in_order(own), precision=HIGH, preferred_element_type=f32)
-    solved = jnp.concatenate(
-        [jnp.where(here == 0, upper, solved[:, :TILE]), solved[:, TILE:]], axis=1
-    )
-    panel = solved.T
-    weight = as_lies(jnp.dot(inverse.T, solved, precision=HIGH, preferred_element_type=f32))
+    upper, inverse = factored(after(corner, low1, high1))
+    low2, high2 = lax.optimization_barrier((low2, high2, far, upper))[:2]
+    low3, high3 = hop(low2, high2)
+    bulk = [picked, low1, low2, low3, None, high3, high2, high1]
 
     names = names.reshape(nz, ny * nc * 16)
     names = jnp.take(names, lax.rem(zi - jnp.arange(nz) + nz, nz), axis=0).reshape(count, 16)
@@ -323,7 +309,9 @@
         def flag(s, t):
             return match[s, t, k][:, None, None]
 
-        got = bulk[k]
+        return pick_slot(bulk[k], flag)
+
+    def pick_slot(got, flag):
         second = jnp.where(flag(1, 0), got[:, 1, 0], got[:, 1, 1])
         return jnp.where(flag(0, 0), got[:, 0, 0], jnp.where(flag(0, 1), got[:, 0, 1], second))
 
@@ -335,12 +323,24 @@
         return table.reshape(4, -1), both.astype(f32) * (1.0 / SCALE)
 
     first_table, first_tiles = batch((0, 1, 7, 2, 6))
+    solved = jnp.dot(inverse, in_order(own), precision=HIGH, preferred_element_type=f32)
+    solved = jnp.concatenate(
+        [jnp.where(here == 0, upper, solved[:, :TILE]), solved[:, TILE:]], axis=1
+    )
+    panel = solved.T
+    weight = as_lies(jnp.dot(inverse.T, solved, precision=HIGH, preferred_element_type=f32)).T
+    low, high = lax.optimization_barrier((bulk[3], bulk[5], weight, first_tiles))[:2]
+    bulk[3], bulk[5] = low, high
+    half = low.shape[0] // 2
+    opposite = jnp.concatenate(
+        [shifted(low[:half], "z", nz, 1), shifted(high[half:], "z", nz, -1)],
+        axis=0,
+    )
     place = (here * 2 - xi * per_range).astype(jnp.int32)[None]
-    weight = after(weight, bulk[3], bulk[5])
     shape = (2 * TILE, per_range * TILE)
     start = first_sum(first_table, place, weight, near, far, first_diag, first_tiles, shape)
     late = [batch((3, 5))]
-    bulk[4] = after(bulk[4], start)
+    bulk[4] = after(opposite, start)
     late.append(batch((4,)))
     last_table = jnp.concatenate([e[0] for e in late], axis=1)
     last_tiles = jnp.concatenate([e[1] for e in late], axis=0)

time: 226 us -> 229 us (1.013)
  waiting for transfers between devices: 48.5 us -> 57.4 us
  local copies, waits for them, and re-layouts: 26 us -> 23.7 us
    ppermute x21, waiting for transfers between devices: 22.9 us -> 29.9 us  [shifted(): return lax.ppermute(value, axis, ring(count, shift))]
    reshape x2, local copies, waits for them, and re-layouts: 2.55 us -> 0.1 us  [as_lies(): value = value.reshape(ny * nz, nc, 2, -1).transpose(1, 0, 2, 3)]
  transfers between devices with their start and end apart: 27 -> 27, of which waited for: 11 -> 12; matrix products, arithmetic and copies ran while one was open for 27% -> 24% of each run, Pallas kernels for 14% -> 13%
where the time goes in v1:
time: 229 us; the launch traced here: 227 us
  starting transfers between devices  68.4 us (30%)
  waiting for transfers between devices  57.4 us (25%)
  Pallas kernels  37.7 us (16%)
  other arithmetic  26.2 us (11%)
  local copies, waits for them, and re-layouts  23.7 us (10%)
  matrix products  12.2 us (5%)
    ppermute x21, starting transfers between devices, shifted(): return lax.ppermute(value, axis, ring(count, shift))  37.4 us
    all_to_all x6, starting transfers between devices, exchanged(): return lax.all_to_all(value, axis, 0, 0, tiled=True)  31 us
    ppermute x21, waiting for transfers between devices, shifted(): return lax.ppermute(value, axis, ring(count, shift))  29.9 us
    all_to_all x6, waiting for transfers between devices, exchanged(): return lax.all_to_all(value, axis, 0, 0, tiled=True)  27.5 us
    pallas_call x1, Pallas kernels, factored(): pl.pallas_call(factor_kernel, out_shape=(shape, shape), scratch_shapes=[p...  15.7 us
    pallas_call x1, Pallas kernels, first_sum(): pl.pallas_call(first_kernel, grid_spec=pltpu.PrefetchScalarGridSpec(num_s...  14 us
    unnamed x4, other arithmetic  8.51 us
    pallas_call x1, Pallas kernels, second_sum(): pl.pallas_call(second_kernel, grid_spec=pltpu.PrefetchScalarGridSpec(num_...  7.99 us
  transfers between devices with their start and end apart: 27, of which 12 were waited for; matrix products, arithmetic and copies ran while one was open for 24% of the time, Pallas kernels for 13%

profile of v1, /device:TPU:1, one launch (start us, length us, event | category | flops | bytes accessed | tf_op | source)
XLA Modules:
  0.0 227.3 jit_solution(4398421089744593302)
XLA Ops:
  0.7 2.5 %fusion.7 = bf16[1024,256]{1,0:T(8,128)(2,1)S(1)} fusion(bf16[2,1024,1024]{2,1,0:T(8,128)(2,1)} %param.4, bf16[2,1024,256]{2,1,0:T(8,128)(2,1)} %param.5), kind=kOutput, calls=%fused_computation.12 | convolution fusion | flops 537133056 | bytes 3145728 | tf_op jit(solution)/shard_map/dot_general | solution.py:188
  3.1 2.1 collective-permute-start
  7.4 2.3 %fusion.10 = bf16[1024,256]{1,0:T(8,128)(2,1)S(1)} fusion(bf16[2,1024,1024]{2,1,0:T(8,128)(2,1)} %param.4, bf16[2,1024,256]{2,1,0:T(8,128)(2,1)S(1)} %copy-done.32), kind=kOutput, calls=%fused_computation.13 | convolution fusion | flops 537133056 | bytes 3145728 | tf_op jit(solution)/shard_map/dot_general | solution.py:188
  9.7 6.2 %collective-permute-done = bf16[1024,256]{1,0:T(8,128)(2,1)S(1)} collective-permute-done((bf16[1024,256]{1,0:T(8,128)(2,1)S(1)}, bf16[1024,256]{1,0:T(8,128)(2,1)S(1)}, u32[]{:S(2)}, u32[]{:S(2)}) %collective-permute-start) | collective-permute-done | bytes 524320 | tf_op jit(solution)/shard_map/ppermute | solution.py:19
  22.4 2.1 collective-permute-done.2
  26.7 2.1 collective-permute-start.5
  30.3 8.1 %all-to-all-start = ((f32[8,8,8,128]{3,2,1,0:T(8,128)}), f32[8,8,8,128]{3,2,1,0:T(8,128)S(1)}, u32[]{:S(2)}, u32[]{:S(2)}) async-start(f32[8,8,8,128]{3,2,1,0:T(8,128)} %bitcast.7), calls=%async_computation | async-start | bytes 524288 | tf_op jit(solution)/shard_map/all_to_all | solution.py:23
  39.1 5.8 %all-to-all-done = f32[8,8,8,128]{3,2,1,0:T(8,128)S(1)} async-done(((f32[8,8,8,128]{3,2,1,0:T(8,128)}), f32[8,8,8,128]{3,2,1,0:T(8,128)S(1)}, u32[]{:S(2)}, u32[]{:S(2)}) %all-to-all-start) | async-done | bytes 262176 | tf_op jit(solution)/shard_map/all_to_all | solution.py:23
  45.6 8.2 %all-to-all-start.1 = ((f32[8,8,8,128]{3,2,1,0:T(8,128)}), f32[8,8,8,128]{3,2,1,0:T(8,128)S(1)}, u32[]{:S(2)}, u32[]{:S(2)}) async-start(f32[8,8,8,128]{3,2,1,0:T(8,128)} %copy.107), calls=%async_computation.1 | async-start | bytes 524288 | tf_op jit(solution)/shard_map/all_to_all | solution.py:23
  59.6 4.4 %all-to-all-done.1 = f32[8,8,8,128]{3,2,1,0:T(8,128)S(1)} async-done(((f32[8,8,8,128]{3,2,1,0:T(8,128)}), f32[8,8,8,128]{3,2,1,0:T(8,128)S(1)}, u32[]{:S(2)}, u32[]{:S(2)}) %all-to-all-start.1) | async-done | bytes 262176 | tf_op jit(solution)/shard_map/all_to_all | solution.py:23
  65.8 3.6 %all-to-all-start.2 = ((f32[8,2,4224]{2,1,0:T(2,128)}), f32[8,2,4224]{2,1,0:T(2,128)S(1)}, u32[]{:S(2)}, u32[]{:S(2)}) async-start(f32[8,2,4224]{2,1,0:T(2,128)} %broadcast_in_dim.456), calls=%async_computation.2 | async-start | bytes 540672 | tf_op jit(solution)/shard_map/all_to_all | solution.py:23
  72.7 5.9 %all-to-all-done.2 = f32[8,2,4224]{2,1,0:T(2,128)S(1)} async-done(((f32[8,2,4224]{2,1,0:T(2,128)}), f32[8,2,4224]{2,1,0:T(2,128)S(1)}, u32[]{:S(2)}, u32[]{:S(2)}) %all-to-all-start.2) | async-done | bytes 270368 | tf_op jit(solution)/shard_map/all_to_all | solution.py:23
  78.7 3.5 %all-to-all-start.3 = ((f16[4,2,2,128,256]{4,3,2,1,0:T(8,128)(2,1)}), f16[4,2,2,128,256]{4,3,2,1,0:T(8,128)(2,1)S(1)}, u32[]{:S(2)}, u32[]{:S(2)}) async-start(f16[4,2,2,128,256]{4,3,2,1,0:T(8,128)(2,1)} %pad_maximum_fusion.1), calls=%async_computation.3 | async-start | bytes 2097152 | tf_op jit(solution)/shard_map/all_to_all | solution.py:23
  83.7 9.6 %all-to-all-done.3 = f16[4,2,2,128,256]{4,3,2,1,0:T(8,128)(2,1)S(1)} async-done(((f16[4,2,2,128,256]{4,3,2,1,0:T(8,128)(2,1)}), f16[4,2,2,128,256]{4,3,2,1,0:T(8,128)(2,1)S(1)}, u32[]{:S(2)}, u32[]{:S(2)}) %all-to-all-start.3) | async-done | bytes 1048608 | tf_op jit(solution)/shard_map/all_to_all | solution.py:23
  94.4 3.5 %all-to-all-start.4 = ((f32[4,16,4224]{2,1,0:T(8,128)}), f32[4,16,4224]{2,1,0:T(8,128)S(1)}, u32[]{:S(2)}, u32[]{:S(2)}) async-start(f32[4,16,4224]{2,1,0:T(8,128)} %broadcast_in_dim.457), calls=%async_computation.4 | async-start | bytes 2162688 | tf_op jit(solution)/shard_map/all_to_all | solution.py:23
  100.8 2.5 %collective-permute-start.10 = (f16[4,2,2,128,256]{4,3,0,2,1:T(8,128)(2,1)}, f16[4,2,2,128,256]{4,3,0,2,1:T(8,128)(2,1)}, u32[]{:S(2)}, u32[]{:S(2)}) collective-permute-start(f16[4,2,2,128,256]{4,3,0,2,1:T(8,128)(2,1)} %copy.113), channel_id=1, source_target_pairs={{0,56},{8,0},{16,8},{24,16},{32,24},{40,32},{48,40},{56,48},{1,57}... | collective-permute-start | bytes 3145736 | tf_op jit(solution)/shard_map/ppermute | solution.py:19
  108.2 6.0 %collective-permute-start.8 = (f32[64,4224]{1,0:T(8,128)S(1)}, f32[64,4224]{1,0:T(8,128)S(1)}, u32[]{:S(2)}, u32[]{:S(2)}) collective-permute-start(f32[64,4224]{1,0:T(8,128)S(1)} %bitcast.291), channel_id=1, source_target_pairs={{0,4},{4,0},{1,5},{5,1},{2,6},{6,2},{3,7},{7,3},{8,12},{12,8},{9,1... | collective-permute-start | bytes 3244040 | tf_op jit(solution)/shard_map/ppermute | solution.py:19
  116.4 4.1 %all-to-all-start.5 = ((f32[4,64,512]{2,1,0:T(8,128)}), f32[4,64,512]{2,1,0:T(8,128)}, u32[]{:S(2)}, u32[]{:S(2)}) async-start(f32[4,64,512]{2,1,0:T(8,128)} %broadcast_in_dim.458), calls=%async_computation.5 | async-start | bytes 1048576 | tf_op jit(solution)/shard_map/all_to_all | solution.py:23
  122.0 2.7 %collective-permute-start.13 = (f16[4,2,2,128,256]{4,3,0,2,1:T(8,128)(2,1)}, f16[4,2,2,128,256]{4,3,0,2,1:T(8,128)(2,1)}, u32[]{:S(2)}, u32[]{:S(2)}) collective-permute-start(f16[4,2,2,128,256]{4,3,0,2,1:T(8,128)(2,1)} %collective-permute-done.10), channel_id=1, source_target_pairs={{0,56},{8,0},{16,8},{24,16},{32,24},{40,32},{48,40},{56,48},{1,57}... | collective-permute-start | bytes 3145736 | tf_op jit(solution)/shard_map/ppermute | solution.py:19
  124.7 2.5 %select_dynamic-update-slice_fusion.1 = (f16[20,128,256]{2,1,0:T(8,128)(2,1)}, f16[40,128,256]{2,1,0:T(8,128)(2,1)}) fusion(f16[20,128,256]{2,1,0:T(8,128)(2,1)} %get-tuple-element.120, pred[4]{0:T(512)(128)(4,1)S(1)} %get-tuple-element.94, pred[4]{0:T(512)(128)(4,1)S(1)} %get-tuple-element.96, pred[4]{0:T(512)(128)(4,1)S(1)} %get-tuple-element.95, ...), kind=kLoop, calls=%fused_computation.79 | loop fusion | flops 786432 | bytes 1572888
  127.2 2.5 %select_dynamic-update-slice_fusion = (f16[20,128,256]{2,1,0:T(8,128)(2,1)}, f16[40,128,256]{2,1,0:T(8,128)(2,1)}) fusion(f16[20,128,256]{2,1,0:T(8,128)(2,1)} %get-tuple-element.118, pred[4]{0:T(512)(128)(4,1)S(1)} %get-tuple-element.91, pred[4]{0:T(512)(128)(4,1)S(1)} %get-tuple-element.92, pred[4]{0:T(512)(128)(4,1)S(1)} %get-tuple-element.93, ...), kind=kLoop, calls=%fused_computation.78 | loop fusion | flops 786432 | bytes 1572888
  131.1 7.1 %collective-permute-start.11 = (f32[64,256]{1,0:T(8,128)S(1)}, f32[64,256]{1,0:T(8,128)S(1)}, u32[]{:S(2)}, u32[]{:S(2)}) collective-permute-start(f32[64,256]{1,0:T(8,128)S(1)} %get-tuple-element.131), channel_id=1, source_target_pairs={{0,4},{4,0},{1,5},{5,1},{2,6},{6,2},{3,7},{7,3},{8,12},{12,8},{9,1... | collective-permute-start | bytes 196616 | tf_op jit(solution)/shard_map/ppermute | solution.py:19
  139.0 15.7 %factored.1 = (f32[128,128]{1,0:T(8,128)}, f32[128,128]{1,0:T(8,128)}) custom-call(f32[128,128]{1,0:T(8,128)} %bitcast.313), custom_call_target="tpu_custom_call" | custom-call | tf_op jit(solution)/shard_map/factored/pallas_call | solution.py:129
  154.7 2.2 fusion.44
  156.9 2.5 %fusion.38 = (f16[20,128,256]{2,1,0:T(8,128)(2,1)}, f16[40,128,256]{2,1,0:T(8,128)(2,1)}) fusion(f16[20,128,256]{2,1,0:T(8,128)(2,1)} %get-tuple-element.114, pred[4]{0:T(512)(128)(4,1)} %get-tuple-element.85, pred[4]{0:T(512)(128)(4,1)} %get-tuple-element.86, pred[4]{0:T(512)(128)(4,1)} %get-tuple-element.87, ...), kind=kLoop, calls=%fused_computation.69 | loop fusion | flops 786432 | bytes 1575936 | tf_op jit(solution)/shard_map/concatenate | solution.py:320
  160.4 2.7 %collective-permute-start.16 = (f16[4,2,2,128,256]{4,3,0,2,1:T(8,128)(2,1)}, f16[4,2,2,128,256]{4,3,0,2,1:T(8,128)(2,1)}, u32[]{:S(2)}, u32[]{:S(2)}) collective-permute-start(f16[4,2,2,128,256]{4,3,0,2,1:T(8,128)(2,1)} %collective-permute-done.13), channel_id=1, source_target_pairs={{0,56},{8,0},{16,8},{24,16},{32,24},{40,32},{48,40},{56,48},{1,57}... | collective-permute-start | bytes 3145736 | tf_op jit(solution)/shard_map/ppermute | solution.py:19
  166.1 2.9 %convert_multiply_fusion.tiles = f32[40,128,256]{2,1,0:T(8,128)} fusion(f16[40,128,256]{2,1,0:T(8,128)(2,1)S(1)} %constant_dynamic-update-slice_fusion.2), kind=kLoop, calls=%fused_computation.1 | loop fusion | flops 2621440 | bytes 7864320 | tf_op jit(solution)/shard_map/mul | solution.py:323
  169.1 17.1 %collective-permute-done.15 = f16[4,2,2,128,256]{4,3,0,2,1:T(8,128)(2,1)} collective-permute-done((f16[4,2,2,128,256]{4,3,0,2,1:T(8,128)(2,1)}, f16[4,2,2,128,256]{4,3,0,2,1:T(8,128)(2,1)}, u32[]{:S(2)}, u32[]{:S(2)}) %collective-permute-start.15) | collective-permute-done | bytes 1048608 | tf_op jit(solution)/shard_map/ppermute | solution.py:19
  187.4 2.5 %collective-permute-start.19 = (f16[2,2,2,128,256]{4,3,0,2,1:T(8,128)(2,1)S(1)}, f16[2,2,2,128,256]{4,3,0,2,1:T(8,128)(2,1)S(1)}, u32[]{:S(2)}, u32[]{:S(2)}) collective-permute-start(f16[2,2,2,128,256]{4,3,0,2,1:T(8,128)(2,1)S(1)} %slice.470), channel_id=1, source_target_pairs={{0,56},{8,0},{16,8},{24,16},{32,24},{40,32},{48,40},{56,48},{1,57}... | collective-permute-start | bytes 1572872 | tf_op jit(solution)/shard_map/ppermute | solution.py:19
  194.9 2.0 collective-permute-start.17
  198.3 14.0 %first_sum.1.start = f32[256,4096]{1,0:T(8,128)} custom-call(s32[4,40]{1,0:T(4,128)} %reshape.355.table, s32[1]{0:T(128)} %bitcast.36.place, f32[256,128]{1,0:T(8,128)} %bitcast.311, f32[64,4224]{1,0:T(8,128)} %bitcast.294, f32[64,4224]{1,0:T(8,128)} %copy-done.2, f32[2,128]{1,0:T(2,128)} %diag.1, f32[40,128,256]{2,1,0:T(8,128)} %convert_multiply_fusion.tiles), custom_call_target="tpu_custom_call" | custom-call | tf_op jit(solution)/shard_map/first_sum/pallas_call | solution.py:146
  219.4 8.0 %second_sum.1 = f32[256,4096]{1,0:T(8,128)} custom-call(s32[4,24]{1,0:T(4,128)} %pad_add_fusion.1.table, f32[256,4096]{1,0:T(8,128)} %first_sum.1.start, f32[24,128,256]{2,1,0:T(8,128)} %pad_maximum_fusion.tiles), custom_call_target="tpu_custom_call" | custom-call | tf_op jit(solution)/shard_map/second_sum/pallas_call | solution.py:166
  (227 shorter events, 58.7 us)
Async XLA Ops:
  3.1 12.8 %collective-permute-start = (bf16[1024,256]{1,0:T(8,128)(2,1)S(1)}, bf16[1024,256]{1,0:T(8,128)(2,1)S(1)}, u32[]{:S(2)}, u32[]{:S(2)}) collective-permute-start(bf16[1024,256]{1,0:T(8,128)(2,1)S(1)} %fusion.7), channel_id=1, source_target_pairs={{0,1},{1,2},{2,3},{3,0},{4,5},{5,6},{6,7},{7,4},{8,9},{9,10},{10,1... | collective-permute-start | bytes 1572872 | tf_op jit(solution)/shard_map/ppermute | solution.py:19
  5.2 12.2 %collective-permute-start.1 = (bf16[1024,256]{1,0:T(8,128)(2,1)S(1)}, bf16[1024,256]{1,0:T(8,128)(2,1)S(1)}, u32[]{:S(2)}, u32[]{:S(2)}) collective-permute-start(bf16[1024,256]{1,0:T(8,128)(2,1)S(1)} %fusion.7), channel_id=1, source_target_pairs={{0,3},{1,0},{2,1},{3,2},{4,7},{5,4},{6,5},{7,6},{8,11},{9,8},{10,9... | collective-permute-start | bytes 1572872 | tf_op jit(solution)/shard_map/ppermute | solution.py:19
  17.5 7.0 %collective-permute-start.2 = (bf16[512,256]{1,0:T(8,128)(2,1)S(1)}, bf16[512,256]{1,0:T(8,128)(2,1)S(1)}, u32[]{:S(2)}, u32[]{:S(2)}) collective-permute-start(bf16[512,256]{1,0:T(8,128)(2,1)S(1)} %slice.372), channel_id=1, source_target_pairs={{0,1},{1,2},{2,3},{3,0},{4,5},{5,6},{6,7},{7,4},{8,9},{9,10},{10,1... | collective-permute-start | bytes 786440 | tf_op jit(solution)/shard_map/ppermute | solution.py:19
  20.1 5.8 %collective-permute-start.3 = (bf16[512,256]{1,0:T(8,128)(2,1)S(1)}, bf16[512,256]{1,0:T(8,128)(2,1)S(1)}, u32[]{:S(2)}, u32[]{:S(2)}) collective-permute-start(bf16[512,256]{1,0:T(8,128)(2,1)S(1)} %slice.373), channel_id=1, source_target_pairs={{0,3},{1,0},{2,1},{3,2},{4,7},{5,4},{6,5},{7,6},{8,11},{9,8},{10,9... | collective-permute-start | bytes 786440 | tf_op jit(solution)/shard_map/ppermute | solution.py:19
  26.0 27.8 %collective-permute-start.4 = (bf16[1024,256]{1,0:T(8,128)(2,1)S(1)}, bf16[1024,256]{1,0:T(8,128)(2,1)S(1)}, u32[]{:S(2)}, u32[]{:S(2)}) collective-permute-start(bf16[1024,256]{1,0:T(8,128)(2,1)S(1)} %fusion.10), channel_id=1, source_target_pairs={{0,1},{1,2},{2,3},{3,0},{4,5},{5,6},{6,7},{7,4},{8,9},{9,10},{10,1... | collective-permute-start | bytes 1572872 | tf_op jit(solution)/shard_map/ppermute | solution.py:19
  26.7 27.1 %collective-permute-start.5 = (bf16[1024,256]{1,0:T(8,128)(2,1)S(1)}, bf16[1024,256]{1,0:T(8,128)(2,1)}, u32[]{:S(2)}, u32[]{:S(2)}) collective-permute-start(bf16[1024,256]{1,0:T(8,128)(2,1)S(1)} %fusion.10), channel_id=1, source_target_pairs={{0,3},{1,0},{2,1},{3,2},{4,7},{5,4},{6,5},{7,6},{8,11},{9,8},{10,9... | collective-permute-start | bytes 1572872 | tf_op jit(solution)/shard_map/ppermute | solution.py:19
  30.3 14.6 %all-to-all-start = ((f32[8,8,8,128]{3,2,1,0:T(8,128)}), f32[8,8,8,128]{3,2,1,0:T(8,128)S(1)}, u32[]{:S(2)}, u32[]{:S(2)}) async-start(f32[8,8,8,128]{3,2,1,0:T(8,128)} %bitcast.7), calls=%async_computation | async-start | bytes 524288 | tf_op jit(solution)/shard_map/all_to_all | solution.py:23
  45.6 18.4 %all-to-all-start.1 = ((f32[8,8,8,128]{3,2,1,0:T(8,128)}), f32[8,8,8,128]{3,2,1,0:T(8,128)S(1)}, u32[]{:S(2)}, u32[]{:S(2)}) async-start(f32[8,8,8,128]{3,2,1,0:T(8,128)} %copy.107), calls=%async_computation.1 | async-start | bytes 524288 | tf_op jit(solution)/shard_map/all_to_all | solution.py:23
  55.4 14.0 %collective-permute-start.7 = (bf16[512,256]{1,0:T(8,128)(2,1)}, bf16[512,256]{1,0:T(8,128)(2,1)}, u32[]{:S(2)}, u32[]{:S(2)}) collective-permute-start(bf16[512,256]{1,0:T(8,128)(2,1)} %slice.383), channel_id=1, source_target_pairs={{0,3},{1,0},{2,1},{3,2},{4,7},{5,4},{6,5},{7,6},{8,11},{9,8},{10,9... | collective-permute-start | bytes 786440 | tf_op jit(solution)/shard_map/ppermute | solution.py:19
  57.8 11.6 %collective-permute-start.6 = (bf16[512,256]{1,0:T(8,128)(2,1)}, bf16[512,256]{1,0:T(8,128)(2,1)}, u32[]{:S(2)}, u32[]{:S(2)}) collective-permute-start(bf16[512,256]{1,0:T(8,128)(2,1)} %slice.382), channel_id=1, source_target_pairs={{0,1},{1,2},{2,3},{3,0},{4,5},{5,6},{6,7},{7,4},{8,9},{9,10},{10,1... | collective-permute-start | bytes 786440 | tf_op jit(solution)/shard_map/ppermute | solution.py:19
  65.8 12.8 %all-to-all-start.2 = ((f32[8,2,4224]{2,1,0:T(2,128)}), f32[8,2,4224]{2,1,0:T(2,128)S(1)}, u32[]{:S(2)}, u32[]{:S(2)}) async-start(f32[8,2,4224]{2,1,0:T(2,128)} %broadcast_in_dim.456), calls=%async_computation.2 | async-start | bytes 540672 | tf_op jit(solution)/shard_map/all_to_all | solution.py:23
  78.7 14.7 %all-to-all-start.3 = ((f16[4,2,2,128,256]{4,3,2,1,0:T(8,128)(2,1)}), f16[4,2,2,128,256]{4,3,2,1,0:T(8,128)(2,1)S(1)}, u32[]{:S(2)}, u32[]{:S(2)}) async-start(f16[4,2,2,128,256]{4,3,2,1,0:T(8,128)(2,1)} %pad_maximum_fusion.1), calls=%async_computation.3 | async-start | bytes 2097152 | tf_op jit(solution)/shard_map/all_to_all | solution.py:23
  94.4 13.9 %all-to-all-start.4 = ((f32[4,16,4224]{2,1,0:T(8,128)}), f32[4,16,4224]{2,1,0:T(8,128)S(1)}, u32[]{:S(2)}, u32[]{:S(2)}) async-start(f32[4,16,4224]{2,1,0:T(8,128)} %broadcast_in_dim.457), calls=%async_computation.4 | async-start | bytes 2162688 | tf_op jit(solution)/shard_map/all_to_all | solution.py:23
  100.6 21.4 %collective-permute-start.9 = (f16[4,2,2,128,256]{4,3,0,2,1:T(8,128)(2,1)}, f16[4,2,2,128,256]{4,3,0,2,1:T(8,128)(2,1)}, u32[]{:S(2)}, u32[]{:S(2)}) collective-permute-start(f16[4,2,2,128,256]{4,3,0,2,1:T(8,128)(2,1)} %copy.113), channel_id=1, source_target_pairs={{0,8},{8,16},{16,24},{24,32},{32,40},{40,48},{48,56},{56,0},{1,9},... | collective-permute-start | bytes 3145736 | tf_op jit(solution)/shard_map/ppermute | solution.py:19
  100.8 21.2 %collective-permute-start.10 = (f16[4,2,2,128,256]{4,3,0,2,1:T(8,128)(2,1)}, f16[4,2,2,128,256]{4,3,0,2,1:T(8,128)(2,1)}, u32[]{:S(2)}, u32[]{:S(2)}) collective-permute-start(f16[4,2,2,128,256]{4,3,0,2,1:T(8,128)(2,1)} %copy.113), channel_id=1, source_target_pairs={{0,56},{8,0},{16,8},{24,16},{32,24},{40,32},{48,40},{56,48},{1,57}... | collective-permute-start | bytes 3145736 | tf_op jit(solution)/shard_map/ppermute | solution.py:19
  108.2 29.9 %collective-permute-start.8 = (f32[64,4224]{1,0:T(8,128)S(1)}, f32[64,4224]{1,0:T(8,128)S(1)}, u32[]{:S(2)}, u32[]{:S(2)}) collective-permute-start(f32[64,4224]{1,0:T(8,128)S(1)} %bitcast.291), channel_id=1, source_target_pairs={{0,4},{4,0},{1,5},{5,1},{2,6},{6,2},{3,7},{7,3},{8,12},{12,8},{9,1... | collective-permute-start | bytes 3244040 | tf_op jit(solution)/shard_map/ppermute | solution.py:19
  116.4 13.8 %all-to-all-start.5 = ((f32[4,64,512]{2,1,0:T(8,128)}), f32[4,64,512]{2,1,0:T(8,128)}, u32[]{:S(2)}, u32[]{:S(2)}) async-start(f32[4,64,512]{2,1,0:T(8,128)} %broadcast_in_dim.458), calls=%async_computation.5 | async-start | bytes 1048576 | tf_op jit(solution)/shard_map/all_to_all | solution.py:23
  122.0 32.7 %collective-permute-start.12 = (f16[4,2,2,128,256]{4,3,0,2,1:T(8,128)(2,1)}, f16[4,2,2,128,256]{4,3,0,2,1:T(8,128)(2,1)S(1)}, u32[]{:S(2)}, u32[]{:S(2)}) collective-permute-start(f16[4,2,2,128,256]{4,3,0,2,1:T(8,128)(2,1)} %collective-permute-done.9), channel_id=1, source_target_pairs={{0,8},{8,16},{16,24},{24,32},{32,40},{40,48},{48,56},{56,0},{1,9},... | collective-permute-start | bytes 3145736 | tf_op jit(solution)/shard_map/ppermute | solution.py:19
  122.0 32.7 %collective-permute-start.13 = (f16[4,2,2,128,256]{4,3,0,2,1:T(8,128)(2,1)}, f16[4,2,2,128,256]{4,3,0,2,1:T(8,128)(2,1)}, u32[]{:S(2)}, u32[]{:S(2)}) collective-permute-start(f16[4,2,2,128,256]{4,3,0,2,1:T(8,128)(2,1)} %collective-permute-done.10), channel_id=1, source_target_pairs={{0,56},{8,0},{16,8},{24,16},{32,24},{40,32},{48,40},{56,48},{1,57}... | collective-permute-start | bytes 3145736 | tf_op jit(solution)/shard_map/ppermute | solution.py:19
  131.1 28.7 %collective-permute-start.11 = (f32[64,256]{1,0:T(8,128)S(1)}, f32[64,256]{1,0:T(8,128)S(1)}, u32[]{:S(2)}, u32[]{:S(2)}) collective-permute-start(f32[64,256]{1,0:T(8,128)S(1)} %get-tuple-element.131), channel_id=1, source_target_pairs={{0,4},{4,0},{1,5},{5,1},{2,6},{6,2},{3,7},{7,3},{8,12},{12,8},{9,1... | collective-permute-start | bytes 196616 | tf_op jit(solution)/shard_map/ppermute | solution.py:19
  159.5 5.0 %collective-permute-start.14 = (f16[20,128,256]{2,1,0:T(8,128)(2,1)}, f16[20,128,256]{2,1,0:T(8,128)(2,1)}, u32[]{:S(2)}, u32[]{:S(2)}) collective-permute-start(f16[20,128,256]{2,1,0:T(8,128)(2,1)} %get-tuple-element.112), channel_id=1, source_target_pairs={{0,4},{4,0},{1,5},{5,1},{2,6},{6,2},{3,7},{7,3},{8,12},{12,8},{9,1... | collective-permute-start | bytes 3932168 | tf_op jit(solution)/shard_map/ppermute | solution.py:19
  160.4 25.9 %collective-permute-start.15 = (f16[4,2,2,128,256]{4,3,0,2,1:T(8,128)(2,1)}, f16[4,2,2,128,256]{4,3,0,2,1:T(8,128)(2,1)}, u32[]{:S(2)}, u32[]{:S(2)}) collective-permute-start(f16[4,2,2,128,256]{4,3,0,2,1:T(8,128)(2,1)} %copy-done.5), channel_id=1, source_target_pairs={{0,8},{8,16},{16,24},{24,32},{32,40},{40,48},{48,56},{56,0},{1,9},... | collective-permute-start | bytes 3145736 | tf_op jit(solution)/shard_map/ppermute | solution.py:19
  160.4 25.8 %collective-permute-start.16 = (f16[4,2,2,128,256]{4,3,0,2,1:T(8,128)(2,1)}, f16[4,2,2,128,256]{4,3,0,2,1:T(8,128)(2,1)}, u32[]{:S(2)}, u32[]{:S(2)}) collective-permute-start(f16[4,2,2,128,256]{4,3,0,2,1:T(8,128)(2,1)} %collective-permute-done.13), channel_id=1, source_target_pairs={{0,56},{8,0},{16,8},{24,16},{32,24},{40,32},{48,40},{56,48},{1,57}... | collective-permute-start | bytes 3145736 | tf_op jit(solution)/shard_map/ppermute | solution.py:19
  169.0 23.9 %copy-start.18 = (pred[4]{0:T(512)(128)(4,1)S(1)}, pred[4]{0:T(512)(128)(4,1)}, u32[]{:S(2)}) copy-start(pred[4]{0:T(512)(128)(4,1)} %get-tuple-element.76) | copy-start | bytes 16
  169.1 23.9 %copy-start.19 = (pred[4]{0:T(512)(128)(4,1)S(1)}, pred[4]{0:T(512)(128)(4,1)}, u32[]{:S(2)}) copy-start(pred[4]{0:T(512)(128)(4,1)} %get-tuple-element.83) | copy-start | bytes 16
  169.1 23.9 %copy-start.20 = (pred[4]{0:T(512)(128)(4,1)S(1)}, pred[4]{0:T(512)(128)(4,1)}, u32[]{:S(2)}) copy-start(pred[4]{0:T(512)(128)(4,1)} %get-tuple-element.84) | copy-start | bytes 16
  169.1 23.9 %copy-start.24 = (pred[4]{0:T(512)(128)(4,1)S(1)}, pred[4]{0:T(512)(128)(4,1)}, u32[]{:S(2)}) copy-start(pred[4]{0:T(512)(128)(4,1)} %get-tuple-element.57) | copy-start | bytes 16
  169.1 23.9 %copy-start.25 = (pred[4]{0:T(512)(128)(4,1)S(1)}, pred[4]{0:T(512)(128)(4,1)}, u32[]{:S(2)}) copy-start(pred[4]{0:T(512)(128)(4,1)} %get-tuple-element.64) | copy-start | bytes 16
  187.4 25.0 %collective-permute-start.19 = (f16[2,2,2,128,256]{4,3,0,2,1:T(8,128)(2,1)S(1)}, f16[2,2,2,128,256]{4,3,0,2,1:T(8,128)(2,1)S(1)}, u32[]{:S(2)}, u32[]{:S(2)}) collective-permute-start(f16[2,2,2,128,256]{4,3,0,2,1:T(8,128)(2,1)S(1)} %slice.470), channel_id=1, source_target_pairs={{0,56},{8,0},{16,8},{24,16},{32,24},{40,32},{48,40},{56,48},{1,57}... | collective-permute-start | bytes 1572872 | tf_op jit(solution)/shard_map/ppermute | solution.py:19
  191.0 21.3 %collective-permute-start.18 = (f16[2,2,2,128,256]{4,3,0,2,1:T(8,128)(2,1)S(1)}, f16[2,2,2,128,256]{4,3,0,2,1:T(8,128)(2,1)}, u32[]{:S(2)}, u32[]{:S(2)}) collective-permute-start(f16[2,2,2,128,256]{4,3,0,2,1:T(8,128)(2,1)S(1)} %slice.469), channel_id=1, source_target_pairs={{0,8},{8,16},{16,24},{24,32},{32,40},{40,48},{48,56},{56,0},{1,9},... | collective-permute-start | bytes 1572872 | tf_op jit(solution)/shard_map/ppermute | solution.py:19
  194.9 21.1 %collective-permute-start.17 = (f16[8,128,256]{2,1,0:T(8,128)(2,1)S(1)}, f16[8,128,256]{2,1,0:T(8,128)(2,1)}, u32[]{:S(2)}, u32[]{:S(2)}) collective-permute-start(f16[8,128,256]{2,1,0:T(8,128)(2,1)S(1)} %pad_maximum_fusion.3), channel_id=1, source_target_pairs={{0,4},{4,0},{1,5},{5,1},{2,6},{6,2},{3,7},{7,3},{8,12},{12,8},{9,1... | collective-permute-start | bytes 1572872 | tf_op jit(solution)/shard_map/ppermute | solution.py:19
  214.3 3.0 %collective-permute-start.20 = (f16[4,128,256]{2,1,0:T(8,128)(2,1)S(1)}, f16[4,128,256]{2,1,0:T(8,128)(2,1)S(1)}, u32[]{:S(2)}, u32[]{:S(2)}) collective-permute-start(f16[4,128,256]{2,1,0:T(8,128)(2,1)S(1)} %get-tuple-element.111), channel_id=1, source_target_pairs={{0,4},{4,0},{1,5},{5,1},{2,6},{6,2},{3,7},{7,3},{8,12},{12,8},{9,1... | collective-permute-start | bytes 786440 | tf_op jit(solution)/shard_map/ppermute | solution.py:19
  (28 other events, 282.5 us)
